TPU v7x, 32 devices: a whole 2x2x4 slice. The times are simulated.
32 devices in a mesh: grp: 2 (over y), row: 4 (over x, core), slab: 4 (over z).
Axes of the slice: x: 2, y: 2, z: 4, core: 2. Of those that a mesh axis runs over, the one named last changes fastest.
Arguments:
- observed: float32 [128, 256, 256], P(('grp', 'slab'), 'row'), parts along dimension 0, may hold values from 0.25 to 4
- band_index: int32 [64], P('slab'), may hold values from 0 to 15
- taps_x: float32 [16, 31], replicated, may hold values from 0.005 to 0.12
- taps_y: float32 [16, 31], replicated, may hold values from 0.005 to 0.12
- taps_z: float32 [31], replicated, may hold values from 0.005 to 0.12
Outputs:
- estimate: float32 [128, 256, 256], P(('grp', 'slab'), 'row'), parts along dimension 0
There are 2 independent parts, one for each index of `grp`. A program takes and returns all parts, laid end to end along the dimension named above; an argument that names none is the same for every part. Nothing has to cross between parts.
All inputs are finite; a program needn't handle non-finite values.
Results may differ from a plain program's by a relative error of at most 0.00015.
Values sent between devices are 32-bit elements; how exact they have to be, the bound alone decides.
A program may use at most 64 MiB of HBM per device.

v0:
```python
import jax
import jax.numpy as jnp
from jax import lax
from jax.sharding import PartitionSpec as P

ITERS = 2


def padded_2(block, sides, width):
    for axis, dim in sides:
        count = lax.axis_size(axis)
        forward = [(i, i + 1) for i in range(count - 1)]
        backward = [(target, source) for source, target in forward]
        low = lax.ppermute(
            lax.slice_in_dim(block, block.shape[dim] - width, None, axis=dim), axis, forward
        )
        high = lax.ppermute(lax.slice_in_dim(block, 0, width, axis=dim), axis, backward)
        block = jnp.concatenate([low, block, high], axis=dim)
    return block


def correlate(padded, taps, dim, length):
    total = None
    for k in range(taps.shape[-1]):
        piece = lax.slice_in_dim(padded, k, k + length, axis=dim)
        if taps.ndim == 2:
            weight = taps[:, k][:, None, None]
        else:
            weight = taps[k]
        term = weight * piece
        total = term if total is None else total + term
    return total


def pad_along(field, radius, dim):
    widths = [(0, 0), (0, 0), (0, 0)]
    widths[dim] = (radius, radius)
    return jnp.pad(field, widths)


def along_rows(field, plane_taps):
    radius = plane_taps.shape[-1] // 2
    padded = padded_2(field, (("row", 1),), radius)
    return correlate(padded, plane_taps, 1, field.shape[1])


def along_depth(field, depth_taps):
    radius = depth_taps.shape[-1] // 2
    padded = padded_2(field, (("slab", 0),), radius)
    return correlate(padded, depth_taps, 0, field.shape[0])


def along_columns(field, plane_taps):
    radius = plane_taps.shape[-1] // 2
    return correlate(pad_along(field, radius, 2), plane_taps, 2, field.shape[2])


def forward(field, plane_x, plane_y, taps_z):
    field = along_rows(field, plane_x)
    field = along_columns(field, plane_y)
    return along_depth(field, taps_z)


def adjoint(field, plane_x, plane_y, taps_z):
    field = along_depth(field, taps_z[::-1])
    field = along_columns(field, plane_y[:, ::-1])
    return along_rows(field, plane_x[:, ::-1])


def on_device(observed, band_index, taps_x, taps_y, taps_z):
    band_count = taps_x.shape[0]
    one_hot = (band_index[:, None] == jnp.arange(band_count, dtype=jnp.int32)[None, :]).astype(
        jnp.float32
    )
    plane_x = jnp.dot(one_hot, taps_x, precision=lax.Precision.HIGHEST)
    plane_y = jnp.dot(one_hot, taps_y, precision=lax.Precision.HIGHEST)
    norm = adjoint(jnp.ones(observed.shape, jnp.float32), plane_x, plane_y, taps_z)
    estimate = observed
    for step in range(ITERS):
        blurred = forward(estimate, plane_x, plane_y, taps_z)
        ratio = observed / blurred
        estimate = estimate * adjoint(ratio, plane_x, plane_y, taps_z) / norm
    return estimate


def solution(mesh):
    in_specs = (P(("grp", "slab"), "row", None), P("slab"), P(), P(), P())
    out_specs = P(("grp", "slab"), "row", None)
    return jax.shard_map(
        on_device, mesh=mesh, in_specs=in_specs, out_specs=out_specs, check_vma=False
    )
```

profile of v0, /device:TPU:0, one launch (start us, length us, event | category | flops | bytes accessed | tf_op | source)
XLA Modules:
  0.0 353.1 jit_solution(15672718708147314349)
XLA Ops:
  0.0 1.2 fusion.1141
  1.2 1.3 collective-permute-start.1
  2.5 3.0 collective-permute-start
  5.6 0.8 fusion.1129
  6.4 0.4 slice_reduce_fusion.58
  6.9 0.5 slice_reduce_fusion.61
  7.6 0.2 fusion.1128
  7.8 0.5 slice_reduce_fusion.60
  8.3 0.4 slice_reduce_fusion.59
  8.7 0.1 constant_dynamic-update-slice_fusion.1
  8.8 0.0 collective-permute-done.1
  8.8 0.0 collective-permute-done
  9.1 4.6 %fusion.367 = f32[16,64,256]{2,1,0:T(8,128)S(1)} fusion(f32[16,64,256]{2,1,0:T(8,128)S(1)} %copy-done.1, f32[16,15,256]{2,1,0:T(8,128)S(1)} %collective-permute-done, f32[16,79,256]{2,1,0:T(8,128)S(1)} %constant_dynamic-update-slice_fusion, f32[16]{0:T(128)S(1)} %get-tuple-element.6, f32[16]{0:T(128)S(1)} %get-tuple-element.7, f32[16]{0:T(128)S(1)} %get-tuple-element.8, ...), kind=kLoop, calls=%fused_computation.1023 | loop fusion | flops 19922944 | bytes 18073536 | tf_op jit(solution)/shard_map/add | solution.py:31
  13.7 9.1 %fusion.458 = f32[16,64,256]{2,1,0:T(8,128)S(1)} fusion(f32[16,64,256]{2,1,0:T(8,128)S(1)} %fusion.367, f32[16]{0:T(128)S(1)} %get-tuple-element.37, f32[16]{0:T(128)S(1)} %get-tuple-element.38, f32[16]{0:T(128)S(1)} %get-tuple-element.39, f32[16]{0:T(128)S(1)} %get-tuple-element.40, f32[16]{0:T(128)S(1)} %get-tuple-element.41, ...), kind=kLoop, calls=%fused_computation.1114 | loop fusion | flops 15990784 | bytes 2099136 | tf_op jit(solution)/shard_map/add | solution.py:31
  22.8 0.0 copy-start.4
  22.8 0.2 fusion.1140
  23.0 5.0 %collective-permute-start.2 = (f32[15,64,256]{2,1,0:T(8,128)S(1)}, f32[15,64,256]{2,1,0:T(8,128)S(1)}, u32[]{:S(2)}, u32[]{:S(2)}) collective-permute-start(f32[15,64,256]{2,1,0:T(8,128)S(1)} %get-tuple-element.83), channel_id=1, source_target_pairs={{0,1},{1,2},{2,3},{4,5},{5,6},{6,7},{8,9},{9,10},{10,11},{12,13},{... | collective-permute-start | bytes 2949128 | tf_op jit(solution)/shard_map/ppermute | solution.py:14
  28.1 1.3 collective-permute-start.3
  29.4 0.1 broadcast.18
  29.4 1.3 collective-permute-start.9
  30.7 6.2 %collective-permute-start.8 = (f32[15,64,256]{2,1,0:T(8,128)S(1)}, f32[15,64,256]{2,1,0:T(8,128)}, u32[]{:S(2)}, u32[]{:S(2)}) collective-permute-start(f32[15,64,256]{2,1,0:T(8,128)S(1)} %broadcast.18), channel_id=1, source_target_pairs={{0,1},{1,2},{2,3},{4,5},{5,6},{6,7},{8,9},{9,10},{10,11},{12,13},{... | collective-permute-start | bytes 2949128 | tf_op jit(solution)/shard_map/ppermute | solution.py:14
  36.9 0.7 fusion.1143
  37.6 0.7 fusion.1142
  38.4 11.6 %collective-permute-done.2 = f32[15,64,256]{2,1,0:T(8,128)S(1)} collective-permute-done((f32[15,64,256]{2,1,0:T(8,128)S(1)}, f32[15,64,256]{2,1,0:T(8,128)S(1)}, u32[]{:S(2)}, u32[]{:S(2)}) %collective-permute-start.2) | collective-permute-done | bytes 983072 | tf_op jit(solution)/shard_map/ppermute | solution.py:14
  50.0 4.6 %collective-permute-done.3 = f32[15,64,256]{2,1,0:T(8,128)S(1)} collective-permute-done((f32[15,64,256]{2,1,0:T(8,128)S(1)}, f32[15,64,256]{2,1,0:T(8,128)S(1)}, u32[]{:S(2)}, u32[]{:S(2)}) %collective-permute-start.3) | collective-permute-done | bytes 983072 | tf_op jit(solution)/shard_map/ppermute | solution.py:17
  54.6 23.8 %fusion.969 = f32[16,64,256]{2,1,0:T(8,128)S(1)} fusion(f32[16,64,256]{2,1,0:T(8,128)S(1)} %copy-done.1, f32[16,64,256]{2,1,0:T(8,128)S(1)} %fusion.458, f32[15,64,256]{2,1,0:T(8,128)S(1)} %collective-permute-done.3, f32[15,64,256]{2,1,0:T(8,128)S(1)} %collective-permute-done.2, f32[]{:T(128)} %bitcast.30, f32[]{:T(128)} %bitcast.29, f32[]{:T(128)} %bitcast.28, ...), kind=kLoop, calls=%fused_computation.1625 | loop fusion | flops 24117248 | bytes 5111932 | tf_op jit(solution)/shard_map/div | solution.py:81
  78.4 0.2 fusion.1139
  78.6 4.4 %collective-permute-start.4 = (f32[15,64,256]{2,1,0:T(8,128)S(1)}, f32[15,64,256]{2,1,0:T(8,128)}, u32[]{:S(2)}, u32[]{:S(2)}) collective-permute-start(f32[15,64,256]{2,1,0:T(8,128)S(1)} %get-tuple-element.81), channel_id=1, source_target_pairs={{0,1},{1,2},{2,3},{4,5},{5,6},{6,7},{8,9},{9,10},{10,11},{12,13},{... | collective-permute-start | bytes 2949128 | tf_op jit(solution)/shard_map/ppermute | solution.py:14
  83.0 1.3 collective-permute-start.5
  84.3 27.5 %fusion.1096 = f32[16,64,256]{2,1,0:T(8,128)S(1)} fusion(f32[15,64,256]{2,1,0:T(8,128)} %collective-permute-done.9, f32[15,64,256]{2,1,0:T(8,128)} %collective-permute-done.8, f32[]{:T(128)} %bitcast.30, f32[]{:T(128)} %bitcast.29, f32[]{:T(128)} %bitcast.28, f32[]{:T(128)} %bitcast.27, f32[]{:T(128)} %bitcast.26, f32[]{:T(128)} %bitcast.25, f32[]{:T(128)} %bitcast.24, ...), kind=kLoop, calls=%fused_computation.1752 | loop fusion | flops 15728640 | bytes 3014780 | tf_op jit(solution)/shard_map/add | solution.py:31
  111.9 9.1 %fusion.578 = f32[16,64,256]{2,1,0:T(8,128)S(1)} fusion(f32[16,64,256]{2,1,0:T(8,128)S(1)} %fusion.1096, f32[16]{0:T(128)S(1)} %get-tuple-element.37, f32[16]{0:T(128)S(1)} %get-tuple-element.38, f32[16]{0:T(128)S(1)} %get-tuple-element.39, f32[16]{0:T(128)S(1)} %get-tuple-element.40, f32[16]{0:T(128)S(1)} %get-tuple-element.41, ...), kind=kLoop, calls=%fused_computation.1234 | loop fusion | flops 15990784 | bytes 2099136 | tf_op jit(solution)/shard_map/add | solution.py:31
  121.0 0.9 fusion.1137
  121.8 1.5 collective-permute-start.10
  123.4 1.3 collective-permute-start.11
  124.7 0.0 collective-permute-done.5
  124.7 27.8 %fusion.882 = f32[16,64,256]{2,1,0:T(8,128)S(1)} fusion(f32[16,64,256]{2,1,0:T(8,128)S(1)} %fusion.969, f32[15,64,256]{2,1,0:T(8,128)} %collective-permute-done.5, f32[15,64,256]{2,1,0:T(8,128)} %collective-permute-done.4, f32[]{:T(128)} %bitcast.30, f32[]{:T(128)} %bitcast.29, f32[]{:T(128)} %bitcast.28, f32[]{:T(128)} %bitcast.27, f32[]{:T(128)} %bitcast.26, ...), kind=kLoop, calls=%fused_computation.1538 | loop fusion | flops 23855104 | bytes 4063356 | tf_op jit(solution)/shard_map/add | solution.py:31
  152.5 9.1 %fusion.518 = f32[16,64,256]{2,1,0:T(8,128)S(1)} fusion(f32[16,64,256]{2,1,0:T(8,128)S(1)} %fusion.882, f32[16]{0:T(128)S(1)} %get-tuple-element.37, f32[16]{0:T(128)S(1)} %get-tuple-element.38, f32[16]{0:T(128)S(1)} %get-tuple-element.39, f32[16]{0:T(128)S(1)} %get-tuple-element.40, f32[16]{0:T(128)S(1)} %get-tuple-element.41, ...), kind=kLoop, calls=%fused_computation.1174 | loop fusion | flops 15990784 | bytes 2099136 | tf_op jit(solution)/shard_map/add | solution.py:31
  161.6 0.0 copy-start.2
  161.7 7.2 %collective-permute-start.6 = (f32[16,15,256]{2,1,0:T(8,128)S(1)}, f32[16,15,256]{2,1,0:T(8,128)}, u32[]{:S(2)}, u32[]{:S(2)}) collective-permute-start(f32[16,15,256]{2,1,0:T(8,128)S(1)} %get-tuple-element.79), channel_id=1, source_target_pairs={{0,4},{4,8},{8,12},{1,5},{5,9},{9,13},{2,6},{6,10},{10,14},{3,7},{... | collective-permute-start | bytes 737288 | tf_op jit(solution)/shard_map/ppermute | solution.py:14
  168.8 1.3 collective-permute-start.7
  170.2 2.7 collective-permute-done.7
  172.9 28.6 %fusion.265 = (f32[16,64,256]{2,1,0:T(8,128)S(1)}, f32[16,64,256]{2,1,0:T(8,128)}) fusion(f32[16,64,256]{2,1,0:T(8,128)S(1)} %copy-done.1, f32[16,64,256]{2,1,0:T(8,128)} %copy-done.2, f32[16,15,256]{2,1,0:T(8,128)} %collective-permute-done.7, f32[16,15,256]{2,1,0:T(8,128)} %collective-permute-done.6, f32[16]{0:T(128)} %copy-done.25, f32[16]{0:T(128)} %copy-done.27, ...), kind=kLoop, calls=%fused_computation.921 | loop fusion | flops 48234496 | bytes 6227904 | tf_op jit(solution)/shard_map/div | solution.py:82
  201.6 6.7 %collective-permute-start.12 = (f32[16,15,256]{2,1,0:T(8,128)S(1)}, f32[16,15,256]{2,1,0:T(8,128)S(1)}, u32[]{:S(2)}, u32[]{:S(2)}) collective-permute-start(f32[16,15,256]{2,1,0:T(8,128)S(1)} %get-tuple-element.75), channel_id=1, source_target_pairs={{0,4},{4,8},{8,12},{1,5},{5,9},{9,13},{2,6},{6,10},{10,14},{3,7},{... | collective-permute-start | bytes 737288 | tf_op jit(solution)/shard_map/ppermute | solution.py:14
  208.2 1.5 collective-permute-start.13
  209.8 1.9 collective-permute-done.13
  211.7 6.3 %fusion.91 = f32[16,64,256]{2,1,0:T(8,128)S(1)} fusion(f32[16,64,256]{2,1,0:T(8,128)S(1)} %get-tuple-element.67, f32[16,15,256]{2,1,0:T(8,128)S(1)} %collective-permute-done.13, f32[16,15,256]{2,1,0:T(8,128)S(1)} %collective-permute-done.12, f32[16]{0:T(128)} %copy-done.25, f32[16]{0:T(128)} %copy-done.27, f32[16]{0:T(128)} %copy-done.29, f32[16]{0:T(128)} %copy-done.31, ...), kind=kLoop, calls=%fused_computation.747 | loop fusion | flops 23855104 | bytes 2590656 | tf_op jit(solution)/shard_map/add | solution.py:31
  218.0 9.1 %fusion.638 = f32[16,64,256]{2,1,0:T(8,128)S(1)} fusion(f32[16,64,256]{2,1,0:T(8,128)S(1)} %fusion.91, f32[16]{0:T(128)S(1)} %get-tuple-element.37, f32[16]{0:T(128)S(1)} %get-tuple-element.38, f32[16]{0:T(128)S(1)} %get-tuple-element.39, f32[16]{0:T(128)S(1)} %get-tuple-element.40, f32[16]{0:T(128)S(1)} %get-tuple-element.41, ...), kind=kLoop, calls=%fused_computation.1294 | loop fusion | flops 15990784 | bytes 2099136 | tf_op jit(solution)/shard_map/add | solution.py:31
  227.1 0.2 fusion.1135
  227.3 4.6 %collective-permute-start.14 = (f32[15,64,256]{2,1,0:T(8,128)S(1)}, f32[15,64,256]{2,1,0:T(8,128)S(1)}, u32[]{:S(2)}, u32[]{:S(2)}) collective-permute-start(f32[15,64,256]{2,1,0:T(8,128)S(1)} %get-tuple-element.73), channel_id=1, source_target_pairs={{0,1},{1,2},{2,3},{4,5},{5,6},{6,7},{8,9},{9,10},{10,11},{12,13},{... | collective-permute-start | bytes 2949128 | tf_op jit(solution)/shard_map/ppermute | solution.py:14
  231.9 1.3 collective-permute-start.15
  233.2 17.5 %collective-permute-done.14 = f32[15,64,256]{2,1,0:T(8,128)S(1)} collective-permute-done((f32[15,64,256]{2,1,0:T(8,128)S(1)}, f32[15,64,256]{2,1,0:T(8,128)S(1)}, u32[]{:S(2)}, u32[]{:S(2)}) %collective-permute-start.14) | collective-permute-done | bytes 983072 | tf_op jit(solution)/shard_map/ppermute | solution.py:14
  250.6 4.7 %collective-permute-done.15 = f32[15,64,256]{2,1,0:T(8,128)S(1)} collective-permute-done((f32[15,64,256]{2,1,0:T(8,128)S(1)}, f32[15,64,256]{2,1,0:T(8,128)S(1)}, u32[]{:S(2)}, u32[]{:S(2)}) %collective-permute-start.15) | collective-permute-done | bytes 983072 | tf_op jit(solution)/shard_map/ppermute | solution.py:17
  255.4 23.8 %fusion.796 = f32[16,64,256]{2,1,0:T(8,128)S(1)} fusion(f32[16,64,256]{2,1,0:T(8,128)S(1)} %copy-done.1, f32[16,64,256]{2,1,0:T(8,128)S(1)} %fusion.638, f32[15,64,256]{2,1,0:T(8,128)S(1)} %collective-permute-done.15, f32[15,64,256]{2,1,0:T(8,128)S(1)} %collective-permute-done.14, f32[]{:T(128)} %bitcast.30, f32[]{:T(128)} %bitcast.29, f32[]{:T(128)} %bitcast.28, ...), kind=kLoop, calls=%fused_computation.1452 | loop fusion | flops 24117248 | bytes 5111932 | tf_op jit(solution)/shard_map/div | solution.py:81
  279.2 0.2 fusion.1134
  279.4 2.6 collective-permute-start.16
  282.0 1.3 collective-permute-start.17
  283.3 18.9 %collective-permute-done.16 = f32[15,64,256]{2,1,0:T(8,128)S(1)} collective-permute-done((f32[15,64,256]{2,1,0:T(8,128)S(1)}, f32[15,64,256]{2,1,0:T(8,128)S(1)}, u32[]{:S(2)}, u32[]{:S(2)}) %collective-permute-start.16) | collective-permute-done | bytes 983072 | tf_op jit(solution)/shard_map/ppermute | solution.py:14
  302.2 4.7 %collective-permute-done.17 = f32[15,64,256]{2,1,0:T(8,128)S(1)} collective-permute-done((f32[15,64,256]{2,1,0:T(8,128)S(1)}, f32[15,64,256]{2,1,0:T(8,128)S(1)}, u32[]{:S(2)}, u32[]{:S(2)}) %collective-permute-start.17) | collective-permute-done | bytes 983072 | tf_op jit(solution)/shard_map/ppermute | solution.py:17
  306.9 23.7 %fusion.709 = f32[16,64,256]{2,1,0:T(8,128)S(1)} fusion(f32[16,64,256]{2,1,0:T(8,128)S(1)} %fusion.796, f32[15,64,256]{2,1,0:T(8,128)S(1)} %collective-permute-done.17, f32[15,64,256]{2,1,0:T(8,128)S(1)} %collective-permute-done.16, f32[]{:T(128)} %bitcast.30, f32[]{:T(128)} %bitcast.29, f32[]{:T(128)} %bitcast.28, f32[]{:T(128)} %bitcast.27, f32[]{:T(128)} %bitcast.26, ...), kind=kLoop, calls=%fused_computation.1365 | loop fusion | flops 23855104 | bytes 4063356 | tf_op jit(solution)/shard_map/add | solution.py:31
  330.9 9.1 %fusion.698 = f32[16,64,256]{2,1,0:T(8,128)S(1)} fusion(f32[16,64,256]{2,1,0:T(8,128)S(1)} %fusion.709, f32[16]{0:T(128)S(1)} %get-tuple-element.37, f32[16]{0:T(128)S(1)} %get-tuple-element.38, f32[16]{0:T(128)S(1)} %get-tuple-element.39, f32[16]{0:T(128)S(1)} %get-tuple-element.40, f32[16]{0:T(128)S(1)} %get-tuple-element.41, ...), kind=kLoop, calls=%fused_computation.1354 | loop fusion | flops 15990784 | bytes 2099136 | tf_op jit(solution)/shard_map/add | solution.py:31
  340.0 3.3 collective-permute-start.18
  343.4 1.3 collective-permute-start.19
  344.7 2.1 collective-permute-done.19
  347.1 6.0 %fusion.5 = f32[16,64,256]{2,1,0:T(8,128)} fusion(f32[16,64,256]{2,1,0:T(8,128)S(1)} %copy-done.3, f32[16,64,256]{2,1,0:T(8,128)S(1)} %get-tuple-element.67, f32[16,64,256]{2,1,0:T(8,128)S(1)} %fusion.698, f32[16,15,256]{2,1,0:T(8,128)S(1)} %collective-permute-done.19, f32[16,15,256]{2,1,0:T(8,128)S(1)} %collective-permute-done.18, f32[16]{0:T(128)S(1)} %copy-done.26, ...), kind=kLoop, calls=%fused_computation.661 | loop fusion | flops 24379392 | bytes 4687808 | tf_op jit(solution)/shard_map/div | solution.py:82
  (136 shorter events, 0.4 us)
Async XLA Ops:
  0.0 5.5 %copy-start = (f32[16,31]{1,0:T(8,128)S(1)}, f32[16,31]{1,0:T(8,128)}, u32[]{:S(2)}) copy-start(f32[16,31]{1,0:T(8,128)} %param.7) | copy-start | bytes 5956
  0.0 8.7 %copy-start.1 = (f32[16,64,256]{2,1,0:T(8,128)S(1)}, f32[16,64,256]{2,1,0:T(8,128)}, u32[]{:S(2)}) copy-start(f32[16,64,256]{2,1,0:T(8,128)} %param.5) | copy-start | bytes 3145732
  0.0 7.4 %copy-start.62 = (s32[16]{0:T(128)S(1)}, s32[16]{0:T(128)}, u32[]{:S(2)}) copy-start(s32[16]{0:T(128)} %param.6) | copy-start | bytes 196
  0.0 7.4 %copy-start.61 = (f32[16,31]{1,0:T(8,128)S(1)}, f32[16,31]{1,0:T(8,128)}, u32[]{:S(2)}) copy-start(f32[16,31]{1,0:T(8,128)} %param.8) | copy-start | bytes 5956
  1.2 7.6 %collective-permute-start.1 = (f32[16,15,256]{2,1,0:T(8,128)S(1)}, f32[16,15,256]{2,1,0:T(8,128)S(1)}, u32[]{:S(2)}, u32[]{:S(2)}) collective-permute-start(f32[16,15,256]{2,1,0:T(8,128)S(1)} %get-tuple-element.85), channel_id=1, source_target_pairs={{4,0},{8,4},{12,8},{5,1},{9,5},{13,9},{6,2},{10,6},{14,10},{7,3},{... | collective-permute-start | bytes 737288 | tf_op jit(solution)/shard_map/ppermute | solution.py:17
  2.5 6.3 %collective-permute-start = (f32[16,15,256]{2,1,0:T(8,128)S(1)}, f32[16,15,256]{2,1,0:T(8,128)S(1)}, u32[]{:S(2)}, u32[]{:S(2)}) collective-permute-start(f32[16,15,256]{2,1,0:T(8,128)S(1)} %get-tuple-element.86), channel_id=1, source_target_pairs={{0,4},{4,8},{8,12},{1,5},{5,9},{9,13},{2,6},{6,10},{10,14},{3,7},{... | collective-permute-start | bytes 737288 | tf_op jit(solution)/shard_map/ppermute | solution.py:14
  6.8 2.1 copy-start.7
  6.8 2.1 copy-start.9
  6.8 2.1 copy-start.11
  6.8 2.1 copy-start.13
  6.8 2.1 copy-start.15
  6.8 2.1 copy-start.17
  6.8 2.1 copy-start.19
  6.8 2.1 copy-start.21
  6.9 6.9 %copy-start.5 = (f32[16]{0:T(128)}, f32[16]{0:T(128)S(1)}, u32[]{:S(2)}) copy-start(f32[16]{0:T(128)S(1)} %get-tuple-element.27) | copy-start | bytes 196
  22.8 14.1 %copy-start.4 = (f32[31]{0:T(128)S(1)}, f32[31]{0:T(128)}, u32[]{:S(2)}) copy-start(f32[31]{0:T(128)} %param.9) | copy-start | bytes 376
  23.0 27.0 %collective-permute-start.2 = (f32[15,64,256]{2,1,0:T(8,128)S(1)}, f32[15,64,256]{2,1,0:T(8,128)S(1)}, u32[]{:S(2)}, u32[]{:S(2)}) collective-permute-start(f32[15,64,256]{2,1,0:T(8,128)S(1)} %get-tuple-element.83), channel_id=1, source_target_pairs={{0,1},{1,2},{2,3},{4,5},{5,6},{6,7},{8,9},{9,10},{10,11},{12,13},{... | collective-permute-start | bytes 2949128 | tf_op jit(solution)/shard_map/ppermute | solution.py:14
  28.1 26.5 %collective-permute-start.3 = (f32[15,64,256]{2,1,0:T(8,128)S(1)}, f32[15,64,256]{2,1,0:T(8,128)S(1)}, u32[]{:S(2)}, u32[]{:S(2)}) collective-permute-start(f32[15,64,256]{2,1,0:T(8,128)S(1)} %get-tuple-element.84), channel_id=1, source_target_pairs={{1,0},{2,1},{3,2},{5,4},{6,5},{7,6},{9,8},{10,9},{11,10},{13,12},{... | collective-permute-start | bytes 2949128 | tf_op jit(solution)/shard_map/ppermute | solution.py:17
  29.4 54.9 %collective-permute-start.9 = (f32[15,64,256]{2,1,0:T(8,128)S(1)}, f32[15,64,256]{2,1,0:T(8,128)}, u32[]{:S(2)}, u32[]{:S(2)}) collective-permute-start(f32[15,64,256]{2,1,0:T(8,128)S(1)} %broadcast.18), channel_id=1, source_target_pairs={{1,0},{2,1},{3,2},{5,4},{6,5},{7,6},{9,8},{10,9},{11,10},{13,12},{... | collective-permute-start | bytes 2949128 | tf_op jit(solution)/shard_map/ppermute | solution.py:17
  30.7 53.6 %collective-permute-start.8 = (f32[15,64,256]{2,1,0:T(8,128)S(1)}, f32[15,64,256]{2,1,0:T(8,128)}, u32[]{:S(2)}, u32[]{:S(2)}) collective-permute-start(f32[15,64,256]{2,1,0:T(8,128)S(1)} %broadcast.18), channel_id=1, source_target_pairs={{0,1},{1,2},{2,3},{4,5},{5,6},{6,7},{8,9},{9,10},{10,11},{12,13},{... | collective-permute-start | bytes 2949128 | tf_op jit(solution)/shard_map/ppermute | solution.py:14
  78.6 46.1 %collective-permute-start.4 = (f32[15,64,256]{2,1,0:T(8,128)S(1)}, f32[15,64,256]{2,1,0:T(8,128)}, u32[]{:S(2)}, u32[]{:S(2)}) collective-permute-start(f32[15,64,256]{2,1,0:T(8,128)S(1)} %get-tuple-element.81), channel_id=1, source_target_pairs={{0,1},{1,2},{2,3},{4,5},{5,6},{6,7},{8,9},{9,10},{10,11},{12,13},{... | collective-permute-start | bytes 2949128 | tf_op jit(solution)/shard_map/ppermute | solution.py:14
  83.0 41.7 %collective-permute-start.5 = (f32[15,64,256]{2,1,0:T(8,128)S(1)}, f32[15,64,256]{2,1,0:T(8,128)}, u32[]{:S(2)}, u32[]{:S(2)}) collective-permute-start(f32[15,64,256]{2,1,0:T(8,128)S(1)} %get-tuple-element.82), channel_id=1, source_target_pairs={{1,0},{2,1},{3,2},{5,4},{6,5},{7,6},{9,8},{10,9},{11,10},{13,12},{... | collective-permute-start | bytes 2949128 | tf_op jit(solution)/shard_map/ppermute | solution.py:17
  121.8 48.3 %collective-permute-start.10 = (f32[16,15,256]{2,1,0:T(8,128)}, f32[16,15,256]{2,1,0:T(8,128)S(1)}, u32[]{:S(2)}, u32[]{:S(2)}) collective-permute-start(f32[16,15,256]{2,1,0:T(8,128)} %get-tuple-element.77), channel_id=1, source_target_pairs={{0,4},{4,8},{8,12},{1,5},{5,9},{9,13},{2,6},{6,10},{10,14},{3,7},{... | collective-permute-start | bytes 737288 | tf_op jit(solution)/shard_map/ppermute | solution.py:14
  123.4 46.8 %collective-permute-start.11 = (f32[16,15,256]{2,1,0:T(8,128)}, f32[16,15,256]{2,1,0:T(8,128)}, u32[]{:S(2)}, u32[]{:S(2)}) collective-permute-start(f32[16,15,256]{2,1,0:T(8,128)} %get-tuple-element.78), channel_id=1, source_target_pairs={{4,0},{8,4},{12,8},{5,1},{9,5},{13,9},{6,2},{10,6},{14,10},{7,3},{... | collective-permute-start | bytes 737288 | tf_op jit(solution)/shard_map/ppermute | solution.py:17
  161.6 8.6 %copy-start.2 = (f32[16,64,256]{2,1,0:T(8,128)}, f32[16,64,256]{2,1,0:T(8,128)S(1)}, u32[]{:S(2)}) copy-start(f32[16,64,256]{2,1,0:T(8,128)S(1)} %fusion.518) | copy-start | bytes 3145732
  161.7 8.5 %collective-permute-start.6 = (f32[16,15,256]{2,1,0:T(8,128)S(1)}, f32[16,15,256]{2,1,0:T(8,128)}, u32[]{:S(2)}, u32[]{:S(2)}) collective-permute-start(f32[16,15,256]{2,1,0:T(8,128)S(1)} %get-tuple-element.79), channel_id=1, source_target_pairs={{0,4},{4,8},{8,12},{1,5},{5,9},{9,13},{2,6},{6,10},{10,14},{3,7},{... | collective-permute-start | bytes 737288 | tf_op jit(solution)/shard_map/ppermute | solution.py:14
  168.8 4.1 %collective-permute-start.7 = (f32[16,15,256]{2,1,0:T(8,128)S(1)}, f32[16,15,256]{2,1,0:T(8,128)}, u32[]{:S(2)}, u32[]{:S(2)}) collective-permute-start(f32[16,15,256]{2,1,0:T(8,128)S(1)} %get-tuple-element.80), channel_id=1, source_target_pairs={{4,0},{8,4},{12,8},{5,1},{9,5},{13,9},{6,2},{10,6},{14,10},{7,3},{... | collective-permute-start | bytes 737288 | tf_op jit(solution)/shard_map/ppermute | solution.py:17
  201.6 8.2 %collective-permute-start.12 = (f32[16,15,256]{2,1,0:T(8,128)S(1)}, f32[16,15,256]{2,1,0:T(8,128)S(1)}, u32[]{:S(2)}, u32[]{:S(2)}) collective-permute-start(f32[16,15,256]{2,1,0:T(8,128)S(1)} %get-tuple-element.75), channel_id=1, source_target_pairs={{0,4},{4,8},{8,12},{1,5},{5,9},{9,13},{2,6},{6,10},{10,14},{3,7},{... | collective-permute-start | bytes 737288 | tf_op jit(solution)/shard_map/ppermute | solution.py:14
  208.2 3.4 collective-permute-start.13
  227.3 23.4 %collective-permute-start.14 = (f32[15,64,256]{2,1,0:T(8,128)S(1)}, f32[15,64,256]{2,1,0:T(8,128)S(1)}, u32[]{:S(2)}, u32[]{:S(2)}) collective-permute-start(f32[15,64,256]{2,1,0:T(8,128)S(1)} %get-tuple-element.73), channel_id=1, source_target_pairs={{0,1},{1,2},{2,3},{4,5},{5,6},{6,7},{8,9},{9,10},{10,11},{12,13},{... | collective-permute-start | bytes 2949128 | tf_op jit(solution)/shard_map/ppermute | solution.py:14
  231.9 23.5 %collective-permute-start.15 = (f32[15,64,256]{2,1,0:T(8,128)S(1)}, f32[15,64,256]{2,1,0:T(8,128)S(1)}, u32[]{:S(2)}, u32[]{:S(2)}) collective-permute-start(f32[15,64,256]{2,1,0:T(8,128)S(1)} %get-tuple-element.74), channel_id=1, source_target_pairs={{1,0},{2,1},{3,2},{5,4},{6,5},{7,6},{9,8},{10,9},{11,10},{13,12},{... | collective-permute-start | bytes 2949128 | tf_op jit(solution)/shard_map/ppermute | solution.py:17
  279.4 22.8 %collective-permute-start.16 = (f32[15,64,256]{2,1,0:T(8,128)S(1)}, f32[15,64,256]{2,1,0:T(8,128)S(1)}, u32[]{:S(2)}, u32[]{:S(2)}) collective-permute-start(f32[15,64,256]{2,1,0:T(8,128)S(1)} %get-tuple-element.71), channel_id=1, source_target_pairs={{0,1},{1,2},{2,3},{4,5},{5,6},{6,7},{8,9},{9,10},{10,11},{12,13},{... | collective-permute-start | bytes 2949128 | tf_op jit(solution)/shard_map/ppermute | solution.py:14
  282.0 24.9 %collective-permute-start.17 = (f32[15,64,256]{2,1,0:T(8,128)S(1)}, f32[15,64,256]{2,1,0:T(8,128)S(1)}, u32[]{:S(2)}, u32[]{:S(2)}) collective-permute-start(f32[15,64,256]{2,1,0:T(8,128)S(1)} %get-tuple-element.72), channel_id=1, source_target_pairs={{1,0},{2,1},{3,2},{5,4},{6,5},{7,6},{9,8},{10,9},{11,10},{13,12},{... | collective-permute-start | bytes 2949128 | tf_op jit(solution)/shard_map/ppermute | solution.py:17
  330.6 16.2 %copy-start.3 = (f32[16,64,256]{2,1,0:T(8,128)S(1)}, f32[16,64,256]{2,1,0:T(8,128)}, u32[]{:S(2)}) copy-start(f32[16,64,256]{2,1,0:T(8,128)} %get-tuple-element.68) | copy-start | bytes 3145732
  330.6 16.2 %copy-start.6 = (f32[16]{0:T(128)S(1)}, f32[16]{0:T(128)}, u32[]{:S(2)}) copy-start(f32[16]{0:T(128)} %copy-done.5) | copy-start | bytes 196
  330.6 16.2 %copy-start.8 = (f32[16]{0:T(128)S(1)}, f32[16]{0:T(128)}, u32[]{:S(2)}) copy-start(f32[16]{0:T(128)} %copy-done.7) | copy-start | bytes 196
  330.7 16.2 %copy-start.10 = (f32[16]{0:T(128)S(1)}, f32[16]{0:T(128)}, u32[]{:S(2)}) copy-start(f32[16]{0:T(128)} %copy-done.9) | copy-start | bytes 196
  330.7 16.2 %copy-start.12 = (f32[16]{0:T(128)S(1)}, f32[16]{0:T(128)}, u32[]{:S(2)}) copy-start(f32[16]{0:T(128)} %copy-done.11) | copy-start | bytes 196
  330.7 16.2 %copy-start.14 = (f32[16]{0:T(128)S(1)}, f32[16]{0:T(128)}, u32[]{:S(2)}) copy-start(f32[16]{0:T(128)} %copy-done.13) | copy-start | bytes 196
  330.7 16.2 %copy-start.16 = (f32[16]{0:T(128)S(1)}, f32[16]{0:T(128)}, u32[]{:S(2)}) copy-start(f32[16]{0:T(128)} %copy-done.15) | copy-start | bytes 196
  330.7 16.2 %copy-start.18 = (f32[16]{0:T(128)S(1)}, f32[16]{0:T(128)}, u32[]{:S(2)}) copy-start(f32[16]{0:T(128)} %copy-done.17) | copy-start | bytes 196
  330.7 16.2 %copy-start.20 = (f32[16]{0:T(128)S(1)}, f32[16]{0:T(128)}, u32[]{:S(2)}) copy-start(f32[16]{0:T(128)} %copy-done.19) | copy-start | bytes 196
  330.7 16.2 %copy-start.22 = (f32[16]{0:T(128)S(1)}, f32[16]{0:T(128)}, u32[]{:S(2)}) copy-start(f32[16]{0:T(128)} %copy-done.21) | copy-start | bytes 196
  330.7 16.2 %copy-start.24 = (f32[16]{0:T(128)S(1)}, f32[16]{0:T(128)}, u32[]{:S(2)}) copy-start(f32[16]{0:T(128)} %copy-done.23) | copy-start | bytes 196
  330.7 16.2 %copy-start.26 = (f32[16]{0:T(128)S(1)}, f32[16]{0:T(128)}, u32[]{:S(2)}) copy-start(f32[16]{0:T(128)} %copy-done.25) | copy-start | bytes 196
  330.7 16.2 %copy-start.28 = (f32[16]{0:T(128)S(1)}, f32[16]{0:T(128)}, u32[]{:S(2)}) copy-start(f32[16]{0:T(128)} %copy-done.27) | copy-start | bytes 196
  330.8 16.2 %copy-start.30 = (f32[16]{0:T(128)S(1)}, f32[16]{0:T(128)}, u32[]{:S(2)}) copy-start(f32[16]{0:T(128)} %copy-done.29) | copy-start | bytes 196
  330.8 16.2 %copy-start.32 = (f32[16]{0:T(128)S(1)}, f32[16]{0:T(128)}, u32[]{:S(2)}) copy-start(f32[16]{0:T(128)} %copy-done.31) | copy-start | bytes 196
  330.8 16.2 %copy-start.34 = (f32[16]{0:T(128)S(1)}, f32[16]{0:T(128)}, u32[]{:S(2)}) copy-start(f32[16]{0:T(128)} %copy-done.33) | copy-start | bytes 196
  330.8 16.2 %copy-start.36 = (f32[16]{0:T(128)S(1)}, f32[16]{0:T(128)}, u32[]{:S(2)}) copy-start(f32[16]{0:T(128)} %copy-done.35) | copy-start | bytes 196
  330.8 16.2 %copy-start.38 = (f32[16]{0:T(128)S(1)}, f32[16]{0:T(128)}, u32[]{:S(2)}) copy-start(f32[16]{0:T(128)} %copy-done.37) | copy-start | bytes 196
  330.8 16.2 %copy-start.40 = (f32[16]{0:T(128)S(1)}, f32[16]{0:T(128)}, u32[]{:S(2)}) copy-start(f32[16]{0:T(128)} %copy-done.39) | copy-start | bytes 196
  330.8 16.2 %copy-start.42 = (f32[16]{0:T(128)S(1)}, f32[16]{0:T(128)}, u32[]{:S(2)}) copy-start(f32[16]{0:T(128)} %copy-done.41) | copy-start | bytes 196
  330.8 16.2 %copy-start.44 = (f32[16]{0:T(128)S(1)}, f32[16]{0:T(128)}, u32[]{:S(2)}) copy-start(f32[16]{0:T(128)} %copy-done.43) | copy-start | bytes 196
  330.8 16.2 %copy-start.46 = (f32[16]{0:T(128)S(1)}, f32[16]{0:T(128)}, u32[]{:S(2)}) copy-start(f32[16]{0:T(128)} %copy-done.45) | copy-start | bytes 196
  330.8 16.2 %copy-start.48 = (f32[16]{0:T(128)S(1)}, f32[16]{0:T(128)}, u32[]{:S(2)}) copy-start(f32[16]{0:T(128)} %copy-done.47) | copy-start | bytes 196
  330.9 16.2 %copy-start.50 = (f32[16]{0:T(128)S(1)}, f32[16]{0:T(128)}, u32[]{:S(2)}) copy-start(f32[16]{0:T(128)} %copy-done.49) | copy-start | bytes 196
  330.9 16.2 %copy-start.52 = (f32[16]{0:T(128)S(1)}, f32[16]{0:T(128)}, u32[]{:S(2)}) copy-start(f32[16]{0:T(128)} %copy-done.51) | copy-start | bytes 196
  330.9 16.2 %copy-start.54 = (f32[16]{0:T(128)S(1)}, f32[16]{0:T(128)}, u32[]{:S(2)}) copy-start(f32[16]{0:T(128)} %copy-done.53) | copy-start | bytes 196
  330.9 16.2 %copy-start.56 = (f32[16]{0:T(128)S(1)}, f32[16]{0:T(128)}, u32[]{:S(2)}) copy-start(f32[16]{0:T(128)} %copy-done.55) | copy-start | bytes 196
  330.9 16.2 %copy-start.58 = (f32[16]{0:T(128)S(1)}, f32[16]{0:T(128)}, u32[]{:S(2)}) copy-start(f32[16]{0:T(128)} %copy-done.57) | copy-start | bytes 196
  330.9 16.2 %copy-start.60 = (f32[16]{0:T(128)S(1)}, f32[16]{0:T(128)}, u32[]{:S(2)}) copy-start(f32[16]{0:T(128)} %copy-done.59) | copy-start | bytes 196
  340.0 4.6 %collective-permute-start.18 = (f32[16,15,256]{2,1,0:T(8,128)S(1)}, f32[16,15,256]{2,1,0:T(8,128)S(1)}, u32[]{:S(2)}, u32[]{:S(2)}) collective-permute-start(f32[16,15,256]{2,1,0:T(8,128)S(1)} %get-tuple-element.69), channel_id=1, source_target_pairs={{0,4},{4,8},{8,12},{1,5},{5,9},{9,13},{2,6},{6,10},{10,14},{3,7},{... | collective-permute-start | bytes 737288 | tf_op jit(solution)/shard_map/ppermute | solution.py:14
  343.4 3.4 collective-permute-start.19
  (19 other events, 28.8 us)
where the time goes:
time: 359 us; the launch traced here: 353 us
  other arithmetic  218 us (61%)
  waiting for transfers between devices  68.8 us (19%)
  starting transfers between devices  57.6 us (16%)
  local copies, waits for them, and re-layouts  6.71 us (2%)
    add x10, other arithmetic, correlate(): total = term if total is None else total + term  135 us
    ppermute x10, waiting for transfers between devices, padded_2(): lax.ppermute(lax.slice_in_dim(block, block.shape[dim] - width, None, axis...  48 us
    div x2, other arithmetic, on_device(): ratio = observed / blurred  47.6 us
    ppermute x10, starting transfers between devices, padded_2(): lax.ppermute(lax.slice_in_dim(block, block.shape[dim] - width, None, axis...  44.5 us
    div x2, other arithmetic, on_device(): estimate = estimate * adjoint(ratio, plane_x, plane_y, taps_z) / norm  34.6 us
    ppermute x10, waiting for transfers between devices, padded_2(): lax.ppermute(lax.slice_in_dim(block, 0, width, axis=dim), axis, backward)  20.8 us
    ppermute x10, starting transfers between devices, padded_2(): lax.ppermute(lax.slice_in_dim(block, 0, width, axis=dim), axis, backward)  13.1 us
  transfers between devices with their start and end apart: 20, of which 9 were waited for; matrix products, arithmetic and copies ran while one was open for 29% of the time, Pallas kernels for 0%

commit v1 on v0

v1 whole, which is shorter than its diff:
```python
import functools

import jax
import jax.numpy as jnp
from jax import lax
from jax.experimental import pallas as pl
from jax.experimental.pallas import tpu as pltpu
from jax.sharding import PartitionSpec as P

ITERS = 2
CHUNK = 16
F32 = jnp.float32
BF16 = jnp.bfloat16


def split(v):
    high = v.astype(BF16)
    return high, (v - high.astype(F32)).astype(BF16)


def chunk_order(count):
    if count < 4:
        return list(range(count))
    return [1, 0, count - 1] + list(range(2, count - 1))


def kernel(
    rows_n, slabs_n, taps,
    band_ref, tz_ref, tzv_ref, txf_ref, txr_ref, tyf_ref, tyr_ref, obs_ref,
    out_ref,
    ext, dext, bz, rz, wf_h, wf_l, wa_h, wa_l, af, aa,
    zs_sem, zr_sem, xs_sem, xr_sem,
):
    depth, height, width = obs_ref.shape
    radius = taps // 2
    halo = CHUNK
    chunks = height // CHUNK
    order = chunk_order(chunks)
    row = lax.axis_index("row")
    slab = lax.axis_index("slab")

    sides = {
        ("row", 0): (row < rows_n - 1, row + 1),
        ("row", 1): (row > 0, row - 1),
        ("slab", 0): (slab < slabs_n - 1, slab + 1),
        ("slab", 1): (slab > 0, slab - 1),
    }

    barrier = pltpu.get_barrier_semaphore()
    for (axis, _), (there, index) in sides.items():
        @pl.when(there)
        def _(axis=axis, index=index):
            pl.semaphore_signal(barrier, inc=1, device_id={axis: index}, device_id_type=pl.DeviceIdType.MESH)

    for (axis, side), buffers in (
        (("row", 1), (ext, dext)), (("row", 0), (ext, dext)),
        (("slab", 1), (bz, rz)), (("slab", 0), (bz, rz)),
    ):
        @pl.when(jnp.logical_not(sides[(axis, side)][0]))
        def _(axis=axis, side=side, buffers=buffers):
            for buffer in buffers:
                for it in range(ITERS):
                    if axis == "row":
                        start = 0 if side == 1 else halo + height
                        buffer[it, :, start:start + halo, :] = jnp.zeros((depth, halo, width), F32)
                    else:
                        start = 0 if side == 1 else radius + depth
                        buffer[it, start:start + radius] = jnp.zeros((radius, height, width), F32)

    pl.semaphore_wait(barrier, sum(there.astype(jnp.int32) for there, _ in sides.values()))

    def row_copy(src, dst, it, which, side):
        if side == 0:
            src_start, dst_start = src[1] + height - halo, 0
        else:
            src_start, dst_start = src[1], halo + height
        return pltpu.make_async_remote_copy(
            src_ref=src[0].at[:, pl.ds(src_start, halo), :],
            dst_ref=dst.at[it, :, pl.ds(dst_start, halo), :],
            send_sem=xs_sem.at[it, which, side],
            recv_sem=xr_sem.at[it, which, side],
            device_id={"row": sides[("row", side)][1]},
            device_id_type=pl.DeviceIdType.MESH,
        )

    def slab_copy(buf, it, which, c, side):
        if side == 0:
            src_start, dst_start = depth, 0
        else:
            src_start, dst_start = radius, radius + depth
        span = pl.ds(c * CHUNK, CHUNK)
        return pltpu.make_async_remote_copy(
            src_ref=buf.at[it, pl.ds(src_start, radius), span, :],
            dst_ref=buf.at[it, pl.ds(dst_start, radius), span, :],
            send_sem=zs_sem.at[it, which, c, side],
            recv_sem=zr_sem.at[it, which, c, side],
            device_id={"slab": sides[("slab", side)][1]},
            device_id_type=pl.DeviceIdType.MESH,
        )

    def start(axis, side, make):
        @pl.when(sides[(axis, side)][0])
        def _():
            make(side).start()

    def recv(axis, side, make):
        @pl.when(sides[(axis, 1 - side)][0])
        def _():
            make(side).wait_recv()

    def sent(axis, side, make):
        @pl.when(sides[(axis, side)][0])
        def _():
            make(side).wait_send()

    sends = []

    def x_make(it, which):
        if which == 0:
            src = (obs_ref, 0) if it == 0 else (ext.at[it], halo)
            return functools.partial(row_copy, src, ext, it, which)
        return functools.partial(row_copy, (dext.at[it], halo), dext, it, which)

    def z_make(it, which, c):
        return functools.partial(slab_copy, bz if which == 0 else rz, it, which, c)

    def x_start(it, which, side):
        start("row", side, x_make(it, which))
        sends.append(("row", side, x_make(it, which)))

    def z_start(it, which, c):
        for side in range(2):
            start("slab", side, z_make(it, which, c))
            sends.append(("slab", side, z_make(it, which, c)))

    def z_recv(it, which, c):
        for side in range(2):
            recv("slab", side, z_make(it, which, c))

    for side in range(2):
        x_start(0, 0, side)

    ext[0, :, halo:halo + height, :] = obs_ref[...]

    kk = 3 * halo

    def build_forward(z, carry):
        band = band_ref[z]
        line = jnp.broadcast_to(tyr_ref[band], (width, width))
        w = pltpu.roll(line, width - radius, 1, stride=1, stride_axis=0)
        near = lax.broadcasted_iota(jnp.int32, (width, width), 0) - lax.broadcasted_iota(jnp.int32, (width, width), 1)
        w = jnp.where((near <= radius) & (near >= -radius), w, 0.0)
        wf_h[z], wf_l[z] = split(w)
        a = jnp.broadcast_to(txf_ref[band], (CHUNK, width))
        a = pltpu.roll(a, halo - radius, 1, stride=1, stride_axis=0)
        high = a.astype(BF16).astype(F32)
        af[z] = (high + pltpu.roll(a - high, kk, 1) + pltpu.roll(high, 2 * kk, 1)).astype(BF16)
        return carry

    def build_adjoint(z, carry):
        band = band_ref[z]
        line = jnp.broadcast_to(tyf_ref[band], (width, width))
        w = pltpu.roll(line, width - radius, 1, stride=1, stride_axis=0)
        near = lax.broadcasted_iota(jnp.int32, (width, width), 0) - lax.broadcasted_iota(jnp.int32, (width, width), 1)
        w = jnp.where((near <= radius) & (near >= -radius), w, 0.0)
        plane = slab * depth + z + radius - lax.broadcasted_iota(jnp.int32, (1, 128), 1)
        inside = (plane >= 0) & (plane < slabs_n * depth)
        cz = jnp.sum(jnp.where(inside, tzv_ref[...], 0.0), axis=1, keepdims=True)
        w = w / (jnp.sum(w, axis=0, keepdims=True) * cz)
        wa_h[z], wa_l[z] = split(w)
        base = jnp.broadcast_to(txr_ref[band], (CHUNK, width))
        base = pltpu.roll(base, halo - radius, 1, stride=1, stride_axis=0)
        for c in range(chunks):
            at = row * height + (c - 1) * CHUNK + lax.broadcasted_iota(jnp.int32, (CHUNK, width), 1)
            inside = (at >= 0) & (at < rows_n * height)
            a = base / jnp.sum(jnp.where(inside, base, 0.0), axis=1, keepdims=True)
            high = a.astype(BF16).astype(F32)
            aa[z, c] = (high + pltpu.roll(a - high, kk, 1) + pltpu.roll(high, 2 * kk, 1)).astype(BF16)
        return carry

    def blur_rows(a, v):
        high, low = split(v)
        return jnp.dot(a[:, :3 * kk], jnp.concatenate([high, high, low], axis=0), preferred_element_type=F32)

    def blur_columns(v, w_h, w_l):
        high, low = split(v)
        n = v.shape[0]
        both = jnp.dot(jnp.concatenate([high, low], axis=0), w_h, preferred_element_type=F32)
        return both[:n] + both[n:] + jnp.dot(high, w_l, preferred_element_type=F32)

    def stage_xy(it, c):
        def body(z, carry):
            v = blur_rows(af[z], ext[it, z, c * CHUNK:c * CHUNK + kk, :])
            bz[it, radius + z, c * CHUNK:(c + 1) * CHUNK, :] = blur_columns(v, wf_h[z], wf_l[z])
            return carry
        lax.fori_loop(0, depth, body, 0, unroll=4)

    def blur_depth(buf, it, tile, lanes, flip):
        total = None
        for k in range(taps):
            weight = tz_ref[taps - 1 - k] if flip else tz_ref[k]
            term = weight * buf[it, k:k + depth, tile, lanes]
            total = term if total is None else total + term
        return total

    def tiles(c):
        for r in range(CHUNK // 8):
            for l in range(width // 128):
                yield slice(c * CHUNK + r * 8, c * CHUNK + r * 8 + 8), slice(l * 128, l * 128 + 128)

    def stage_ratio(it, c):
        for tile, lanes in tiles(c):
            rz[it, radius:radius + depth, tile, lanes] = obs_ref[:, tile, lanes] / blur_depth(bz, it, tile, lanes, False)

    def stage_zy(it, c):
        inner = slice(halo + c * CHUNK, halo + (c + 1) * CHUNK)
        for tile, lanes in tiles(c):
            target = slice(halo + tile.start, halo + tile.stop)
            dext[it, :, target, lanes] = blur_depth(rz, it, tile, lanes, True)

        def body(z, carry):
            dext[it, z, inner, :] = blur_columns(dext[it, z, inner, :], wa_h[z], wa_l[z])
            return carry
        lax.fori_loop(0, depth, body, 0, unroll=4)

    def stage_x(it, c):
        span = slice(c * CHUNK, (c + 1) * CHUNK)
        inner = slice(halo + c * CHUNK, halo + (c + 1) * CHUNK)

        def body(z, carry):
            v = ext[it, z, inner, :] * blur_rows(aa[z, c], dext[it, z, c * CHUNK:c * CHUNK + kk, :])
            if it == ITERS - 1:
                out_ref[z, span, :] = v
            else:
                ext[it + 1, z, inner, :] = v
            return carry
        lax.fori_loop(0, depth, body, 0, unroll=4)

    lax.fori_loop(0, depth, build_forward, 0)
    for it in range(ITERS):
        for c in order:
            if c == 0:
                recv("row", 0, x_make(it, 0))
            if c == chunks - 1:
                recv("row", 1, x_make(it, 0))
            stage_xy(it, c)
            z_start(it, 0, c)
        if it == 0:
            lax.fori_loop(0, depth, build_adjoint, 0)
        for c in order:
            z_recv(it, 0, c)
            stage_ratio(it, c)
            z_start(it, 1, c)
        for c in order:
            z_recv(it, 1, c)
            stage_zy(it, c)
            if c == 0:
                x_start(it, 1, 1)
            if c == chunks - 1:
                x_start(it, 1, 0)
        for c in [0, chunks - 1] + list(range(1, chunks - 1)):
            if c == 0:
                recv("row", 0, x_make(it, 1))
            if c == chunks - 1:
                recv("row", 1, x_make(it, 1))
            stage_x(it, c)
            if it < ITERS - 1:
                if c == 0:
                    x_start(it + 1, 0, 1)
                if c == chunks - 1:
                    x_start(it + 1, 0, 0)

    for axis, side, make in sends:
        sent(axis, side, make)


def solution(mesh):
    rows_n, slabs_n = mesh.shape["row"], mesh.shape["slab"]

    def on_device(observed, band_index, taps_x, taps_y, taps_z):
        depth, height, width = observed.shape
        bands, taps = taps_x.shape
        radius = taps // 2

        def padded(t):
            return jnp.pad(t, ((0, 0), (0, width - taps)))[:, None, :]

        tzv = jnp.pad(taps_z, (0, 128 - taps))[None, :]
        vmem = pl.BlockSpec(memory_space=pltpu.VMEM)
        smem = pl.BlockSpec(memory_space=pltpu.SMEM)
        chunks = height // CHUNK
        return pl.pallas_call(
            functools.partial(kernel, rows_n, slabs_n, taps),
            out_shape=jax.ShapeDtypeStruct(observed.shape, F32),
            in_specs=[smem, smem] + [vmem] * 6,
            out_specs=vmem,
            scratch_shapes=[
                pltpu.VMEM((ITERS, depth, height + 2 * CHUNK, width), F32),
                pltpu.VMEM((ITERS, depth, height + 2 * CHUNK, width), F32),
                pltpu.VMEM((ITERS, depth + 2 * radius, height, width), F32),
                pltpu.VMEM((ITERS, depth + 2 * radius, height, width), F32),
                pltpu.VMEM((depth, width, width), BF16),
                pltpu.VMEM((depth, width, width), BF16),
                pltpu.VMEM((depth, width, width), BF16),
                pltpu.VMEM((depth, width, width), BF16),
                pltpu.VMEM((depth, CHUNK, width), BF16),
                pltpu.VMEM((depth, chunks, CHUNK, width), BF16),
                pltpu.SemaphoreType.DMA((ITERS, 2, chunks, 2)),
                pltpu.SemaphoreType.DMA((ITERS, 2, chunks, 2)),
                pltpu.SemaphoreType.DMA((ITERS, 2, 2)),
                pltpu.SemaphoreType.DMA((ITERS, 2, 2)),
            ],
            compiler_params=pltpu.CompilerParams(
                collective_id=0, has_side_effects=True, vmem_limit_bytes=60 * 1024 * 1024
            ),
        )(
            band_index, taps_z, tzv,
            padded(taps_x), padded(taps_x[:, ::-1]), padded(taps_y), padded(taps_y[:, ::-1]),
            observed,
        )

    in_specs = (P(("grp", "slab"), "row", None), P("slab"), P(), P(), P())
    return jax.shard_map(
        on_device, mesh=mesh, in_specs=in_specs, out_specs=P(("grp", "slab"), "row", None), check_vma=False
    )
```

time: 359 us -> 118 us (0.33); the launches traced: 353 us -> 117 us
  other arithmetic: 218 us -> 0 us
  Pallas kernels: 0 us -> 110 us
  waiting for transfers between devices: 68.8 us -> 0 us
  starting transfers between devices: 57.6 us -> 0 us
    add x10 -> x0, other arithmetic: 135 us -> none  [correlate(): total = term if total is None else total + term]
    pallas_call x0 -> x1, Pallas kernels: none -> 110 us  [on_device(): pl.pallas_call(functools.partial(kernel, rows_n, slabs_n, taps), out_shap...]
    div x4 -> x0, other arithmetic: 82.2 us -> none  [the longest x2 47.6 us: on_device(): ratio = observed / blurred]
    ppermute x20 -> x0, waiting for transfers between devices: 68.8 us -> none  [the longest x10 48 us: padded_2(): lax.ppermute(lax.slice_in_dim(block, block.shape[dim] - width, None, axis...]
    ppermute x20 -> x0, starting transfers between devices: 57.6 us -> none  [the longest x10 44.5 us: padded_2(): lax.ppermute(lax.slice_in_dim(block, block.shape[dim] - width, None, axis...]
    slice x15 -> x0, local copies, waits for them, and re-layouts: 6.24 us -> none  [the longest x8 1.85 us: padded_2(): lax.slice_in_dim(block, block.shape[dim] - width, None, axis=dim)]
    broadcast_in_dim x0 -> x5, local copies, waits for them, and re-layouts: none -> 3.7 us  [the longest x4 2.47 us: padded(): return jnp.pad(t, ((0, 0), (0, width - taps)))[:, None, :]]
  transfers between devices with their start and end apart: 20 -> 0, of which waited for: 9 -> 0; matrix products, arithmetic and copies ran while one was open for 29% -> 0% of each run, Pallas kernels for 0% -> 0%
where the time goes in v1:
time: 118 us; the launch traced here: 117 us
  Pallas kernels  110 us (93%)
  local copies, waits for them, and re-layouts  7.02 us (6%)
    pallas_call x1, Pallas kernels, on_device(): pl.pallas_call(functools.partial(kernel, rows_n, slabs_n, taps), out_shap...  110 us
    broadcast_in_dim x4, local copies, waits for them, and re-layouts, padded(): return jnp.pad(t, ((0, 0), (0, width - taps)))[:, None, :]  2.47 us
    unnamed x5, local copies, waits for them, and re-layouts  2.45 us

profile of v1, /device:TPU:0, one launch (start us, length us, event | category | flops | bytes accessed | tf_op | source)
XLA Modules:
  0.0 117.2 jit_solution(2357406584484483335)
XLA Ops:
  0.0 1.2 %pad_bitcast_fusion.tzv_ref = f32[1,128]{1,0:T(1,128)} fusion(f32[31]{0:T(128)} %tz_ref.1), kind=kLoop, calls=%fused_computation | loop fusion | bytes 636 | tf_op jit(solution)/shard_map/broadcast_in_dim | solution.py:288
  1.2 0.8 rev.6
  2.0 0.0 copy-start.1
  2.0 0.6 broadcast_in_dim.17.txr_ref
  2.6 0.1 copy-done.1
  2.7 0.1 rev.7
  2.8 0.0 copy-start
  2.8 0.6 broadcast_in_dim.19.tyr_ref
  3.4 0.1 copy-done
  3.5 0.6 broadcast_in_dim.16.txf_ref
  4.1 0.6 broadcast_in_dim.18.tyf_ref
  4.7 110.2 %shard_map.55 = f32[16,64,256]{2,1,0:T(8,128)} custom-call(s32[16]{0:T(128)} %band_ref.1, f32[31]{0:T(128)} %tz_ref.1, f32[1,128]{1,0:T(1,128)} %pad_bitcast_fusion.tzv_ref, f32[16,1,256]{2,1,0:T(1,128)} %broadcast_in_dim.16.txf_ref, f32[16,1,256]{2,1,0:T(1,128)} %broadcast_in_dim.17.txr_ref, f32[16,1,256]{2,1,0:T(1,128)} %broadcast_in_dim.18.tyf_ref, ...), custom_call_target="tpu_custom_call" | custom-call | tf_op jit(solution)/shard_map/pallas_call | solution.py:292
  114.9 2.3 %copy.7 = f32[16,64,256]{2,1,0:T(8,128)} copy(f32[16,64,256]{2,1,0:T(8,128)} %shard_map.55) | data formatting | bytes 2097152
  (4 shorter events, 0.0 us)
Async XLA Ops:
  2.0 0.7 copy-start.1
  2.8 0.7 copy-start

commit v2 on v1

--- a/solution.py
+++ b/solution.py
@@ -9,6 +9,7 @@
 
 ITERS = 2
 CHUNK = 16
+LANES = 128
 F32 = jnp.float32
 BF16 = jnp.bfloat16
 
@@ -26,9 +27,9 @@
 
 def kernel(
     rows_n, slabs_n, taps,
-    band_ref, tz_ref, tzv_ref, txf_ref, txr_ref, tyf_ref, tyr_ref, obs_ref,
+    band_ref, tz_ref, tx_ref, ty_ref, obs_ref,
     out_ref,
-    ext, dext, bz, rz, wf_h, wf_l, wa_h, wa_l, af, aa,
+    txf_ref, txr_ref, tyf_ref, tyr_ref, ext, dext, bz, rz, wf_h, wf_l, wa_h, wa_l, af, aa,
     zs_sem, zr_sem, xs_sem, xr_sem,
 ):
     depth, height, width = obs_ref.shape
@@ -52,20 +53,16 @@
         def _(axis=axis, index=index):
             pl.semaphore_signal(barrier, inc=1, device_id={axis: index}, device_id_type=pl.DeviceIdType.MESH)
 
-    for (axis, side), buffers in (
-        (("row", 1), (ext, dext)), (("row", 0), (ext, dext)),
-        (("slab", 1), (bz, rz)), (("slab", 0), (bz, rz)),
-    ):
-        @pl.when(jnp.logical_not(sides[(axis, side)][0]))
-        def _(axis=axis, side=side, buffers=buffers):
-            for buffer in buffers:
-                for it in range(ITERS):
-                    if axis == "row":
-                        start = 0 if side == 1 else halo + height
-                        buffer[it, :, start:start + halo, :] = jnp.zeros((depth, halo, width), F32)
-                    else:
-                        start = 0 if side == 1 else radius + depth
-                        buffer[it, start:start + radius] = jnp.zeros((radius, height, width), F32)
+    def clear(axis, buffer, it):
+        for side in range(2):
+            @pl.when(jnp.logical_not(sides[(axis, side)][0]))
+            def _():
+                if axis == "row":
+                    first = 0 if side == 1 else halo + height
+                    buffer[it, :, first:first + halo, :] = jnp.zeros((depth, halo, width), F32)
+                else:
+                    first = 0 if side == 1 else radius + depth
+                    buffer[it, first:first + radius] = jnp.zeros((radius, height, width), F32)
 
     pl.semaphore_wait(barrier, sum(there.astype(jnp.int32) for there, _ in sides.values()))
 
@@ -143,39 +140,74 @@
     ext[0, :, halo:halo + height, :] = obs_ref[...]
 
     kk = 3 * halo
+    mirror = (
+        lax.broadcasted_iota(jnp.int32, (LANES, LANES), 0) + lax.broadcasted_iota(jnp.int32, (LANES, LANES), 1)
+        == taps - 1
+    ).astype(F32)
+    for source, ahead, back in ((tx_ref, txf_ref, txr_ref), (ty_ref, tyf_ref, tyr_ref)):
+        ahead[...] = jnp.zeros(ahead.shape, F32)
+        ahead[:, 0:taps] = source[...]
+        back[...] = jnp.dot(ahead[...], mirror, precision=lax.Precision.HIGHEST, preferred_element_type=F32)
+
+    gap = lax.broadcasted_iota(jnp.int32, (LANES, LANES), 0) - lax.broadcasted_iota(jnp.int32, (LANES, LANES), 1)
+    blocks = range(width // LANES)
+
+    def column_band(line):
+        ring = pltpu.roll(jnp.broadcast_to(line, (LANES, LANES)), LANES - radius, 1, stride=1, stride_axis=0)
+
+        def block(offset):
+            near = gap + offset * LANES
+            return jnp.where((near <= radius) & (near >= -radius), ring, 0.0)
+        made = {offset: block(offset) for offset in (-1, 0, 1)}
+        return [[made.get(i - j) for j in blocks] for i in blocks]
+
+    def store_band(w_h, w_l, z, band, scale):
+        for i in blocks:
+            for j in blocks:
+                part = jnp.zeros((LANES, LANES), F32) if band[i][j] is None else band[i][j]
+                if scale is not None:
+                    part = part * scale[j]
+                high, low = split(part)
+                w_h[z, i * LANES:(i + 1) * LANES, j * LANES:(j + 1) * LANES] = high
+                w_l[z, i * LANES:(i + 1) * LANES, j * LANES:(j + 1) * LANES] = low
+
+    def store_rows(a):
+        high = a.astype(BF16).astype(F32)
+        low = a - high
+        zero = jnp.zeros(a.shape, F32)
+        first = jnp.concatenate([high, zero], axis=1)
+        second = jnp.concatenate([low, zero], axis=1)
+        return (first + pltpu.roll(second, kk, 1) + pltpu.roll(first, 2 * kk, 1)).astype(BF16)
+
+    def row_band(line):
+        return pltpu.roll(jnp.broadcast_to(line, (CHUNK, LANES)), halo - radius, 1, stride=1, stride_axis=0)
 
     def build_forward(z, carry):
-        band = band_ref[z]
-        line = jnp.broadcast_to(tyr_ref[band], (width, width))
-        w = pltpu.roll(line, width - radius, 1, stride=1, stride_axis=0)
-        near = lax.broadcasted_iota(jnp.int32, (width, width), 0) - lax.broadcasted_iota(jnp.int32, (width, width), 1)
-        w = jnp.where((near <= radius) & (near >= -radius), w, 0.0)
-        wf_h[z], wf_l[z] = split(w)
-        a = jnp.broadcast_to(txf_ref[band], (CHUNK, width))
-        a = pltpu.roll(a, halo - radius, 1, stride=1, stride_axis=0)
-        high = a.astype(BF16).astype(F32)
-        af[z] = (high + pltpu.roll(a - high, kk, 1) + pltpu.roll(high, 2 * kk, 1)).astype(BF16)
+        at = pl.ds(band_ref[z], 1)
+        store_band(wf_h, wf_l, z, column_band(tyr_ref[at, :]), None)
+        af[z] = store_rows(row_band(txf_ref[at, :]))
         return carry
 
     def build_adjoint(z, carry):
-        band = band_ref[z]
-        line = jnp.broadcast_to(tyf_ref[band], (width, width))
-        w = pltpu.roll(line, width - radius, 1, stride=1, stride_axis=0)
-        near = lax.broadcasted_iota(jnp.int32, (width, width), 0) - lax.broadcasted_iota(jnp.int32, (width, width), 1)
-        w = jnp.where((near <= radius) & (near >= -radius), w, 0.0)
-        plane = slab * depth + z + radius - lax.broadcasted_iota(jnp.int32, (1, 128), 1)
+        at = pl.ds(band_ref[z], 1)
+        band = column_band(tyf_ref[at, :])
+        lane = lax.broadcasted_iota(jnp.int32, (1, LANES), 1)
+        tzv = jnp.zeros((1, LANES), F32)
+        for k in range(taps):
+            tzv = jnp.where(lane == k, tz_ref[k], tzv)
+        plane = slab * depth + z + radius - lane
         inside = (plane >= 0) & (plane < slabs_n * depth)
-        cz = jnp.sum(jnp.where(inside, tzv_ref[...], 0.0), axis=1, keepdims=True)
-        w = w / (jnp.sum(w, axis=0, keepdims=True) * cz)
-        wa_h[z], wa_l[z] = split(w)
-        base = jnp.broadcast_to(txr_ref[band], (CHUNK, width))
-        base = pltpu.roll(base, halo - radius, 1, stride=1, stride_axis=0)
+        cz = jnp.sum(jnp.where(inside, tzv, 0.0), axis=1, keepdims=True)
+        scale = []
+        for j in blocks:
+            total = sum(jnp.sum(band[i][j], axis=0, keepdims=True) for i in blocks if band[i][j] is not None)
+            scale.append(1.0 / (total * cz))
+        store_band(wa_h, wa_l, z, band, scale)
+        base = row_band(txr_ref[at, :])
         for c in range(chunks):
-            at = row * height + (c - 1) * CHUNK + lax.broadcasted_iota(jnp.int32, (CHUNK, width), 1)
-            inside = (at >= 0) & (at < rows_n * height)
-            a = base / jnp.sum(jnp.where(inside, base, 0.0), axis=1, keepdims=True)
-            high = a.astype(BF16).astype(F32)
-            aa[z, c] = (high + pltpu.roll(a - high, kk, 1) + pltpu.roll(high, 2 * kk, 1)).astype(BF16)
+            at_row = row * height + (c - 1) * CHUNK + lax.broadcasted_iota(jnp.int32, (CHUNK, LANES), 1)
+            inside = (at_row >= 0) & (at_row < rows_n * height)
+            aa[z, c] = store_rows(base / jnp.sum(jnp.where(inside, base, 0.0), axis=1, keepdims=True))
         return carry
 
     def blur_rows(a, v):
@@ -236,33 +268,17 @@
             return carry
         lax.fori_loop(0, depth, body, 0, unroll=4)
 
-    lax.fori_loop(0, depth, build_forward, 0)
+    clear("row", ext, 0)
+    lax.fori_loop(0, depth, build_forward, 0, unroll=2)
     for it in range(ITERS):
-        for c in order:
+        def edge_x(which, c, it=it):
             if c == 0:
-                recv("row", 0, x_make(it, 0))
+                recv("row", 0, x_make(it, which))
             if c == chunks - 1:
-                recv("row", 1, x_make(it, 0))
-            stage_xy(it, c)
-            z_start(it, 0, c)
-        if it == 0:
-            lax.fori_loop(0, depth, build_adjoint, 0)
-        for c in order:
-            z_recv(it, 0, c)
-            stage_ratio(it, c)
-            z_start(it, 1, c)
-        for c in order:
-            z_recv(it, 1, c)
-            stage_zy(it, c)
-            if c == 0:
-                x_start(it, 1, 1)
-            if c == chunks - 1:
-                x_start(it, 1, 0)
-        for c in [0, chunks - 1] + list(range(1, chunks - 1)):
-            if c == 0:
-                recv("row", 0, x_make(it, 1))
-            if c == chunks - 1:
-                recv("row", 1, x_make(it, 1))
+                recv("row", 1, x_make(it, which))
+
+        def back_x(c, it=it, edge_x=edge_x):
+            edge_x(1, c)
             stage_x(it, c)
             if it < ITERS - 1:
                 if c == 0:
@@ -270,6 +286,50 @@
                 if c == chunks - 1:
                     x_start(it + 1, 0, 0)
 
+        for n, c in enumerate(order):
+            edge_x(0, c)
+            stage_xy(it, c)
+            z_start(it, 0, c)
+            if n == 0 and it > 0:
+                for extra in late:
+                    late_x(extra)
+        if it == 0:
+            lax.fori_loop(0, depth, build_adjoint, 0)
+            for buffer in (bz, rz):
+                for i in range(ITERS):
+                    clear("slab", buffer, i)
+            for i in range(ITERS):
+                clear("row", dext, i)
+            for i in range(1, ITERS):
+                clear("row", ext, i)
+        for c in order:
+            z_recv(it, 0, c)
+            stage_ratio(it, c)
+            z_start(it, 1, c)
+        done, left = [], list(range(chunks))
+        for n, c in enumerate(order):
+            if n == chunks - 1:
+                for e in list(left):
+                    if all(near in done for near in (e - 1, e, e + 1) if 0 <= near < chunks):
+                        back_x(e)
+                        left.remove(e)
+            z_recv(it, 1, c)
+            stage_zy(it, c)
+            done.append(c)
+            if c == 0:
+                x_start(it, 1, 1)
+            if c == chunks - 1:
+                x_start(it, 1, 0)
+        needed = [e for e in left if abs(e - order[0]) <= 1]
+        late = [e for e in left if e not in needed]
+        late_x = back_x
+        for e in needed:
+            back_x(e)
+        if it == ITERS - 1 or order[0] in (0, chunks - 1):
+            for e in late:
+                back_x(e)
+            late = []
+
     for axis, side, make in sends:
         sent(axis, side, make)
 
@@ -282,19 +342,15 @@
         bands, taps = taps_x.shape
         radius = taps // 2
 
-        def padded(t):
-            return jnp.pad(t, ((0, 0), (0, width - taps)))[:, None, :]
-
-        tzv = jnp.pad(taps_z, (0, 128 - taps))[None, :]
         vmem = pl.BlockSpec(memory_space=pltpu.VMEM)
         smem = pl.BlockSpec(memory_space=pltpu.SMEM)
         chunks = height // CHUNK
         return pl.pallas_call(
             functools.partial(kernel, rows_n, slabs_n, taps),
             out_shape=jax.ShapeDtypeStruct(observed.shape, F32),
-            in_specs=[smem, smem] + [vmem] * 6,
+            in_specs=[smem, smem] + [vmem] * 3,
             out_specs=vmem,
-            scratch_shapes=[
+            scratch_shapes=[pltpu.VMEM((bands, LANES), F32)] * 4 + [
                 pltpu.VMEM((ITERS, depth, height + 2 * CHUNK, width), F32),
                 pltpu.VMEM((ITERS, depth, height + 2 * CHUNK, width), F32),
                 pltpu.VMEM((ITERS, depth + 2 * radius, height, width), F32),
@@ -311,11 +367,10 @@
                 pltpu.SemaphoreType.DMA((ITERS, 2, 2)),
             ],
             compiler_params=pltpu.CompilerParams(
-                collective_id=0, has_side_effects=True, vmem_limit_bytes=60 * 1024 * 1024
+                collective_id=0, has_side_effects=True, vmem_limit_bytes=40 * 1024 * 1024
             ),
         )(
-            band_index, taps_z, tzv,
-            padded(taps_x), padded(taps_x[:, ::-1]), padded(taps_y), padded(taps_y[:, ::-1]),
+            band_index, taps_z, taps_x, taps_y,
             observed,
         )
 

time: 118 us -> 111 us (0.941)
  Pallas kernels: 110 us -> 106 us
  local copies, waits for them, and re-layouts: 7.02 us -> 4.9 us
    pallas_call x1, Pallas kernels: 110 us -> 106 us  [on_device(): pl.pallas_call(functools.partial(kernel, rows_n, slabs_n, taps), out_shap...]
    broadcast_in_dim x5 -> x0, local copies, waits for them, and re-layouts: 3.7 us -> none  [the longest x4 2.47 us: padded(): return jnp.pad(t, ((0, 0), (0, width - taps)))[:, None, :]]
    unnamed x5 -> x11, local copies, waits for them, and re-layouts: 2.45 us -> 4.9 us
where the time goes in v2:
time: 111 us
  Pallas kernels  106 us (95%)
  local copies, waits for them, and re-layouts  4.9 us (4%)
    pallas_call x1, Pallas kernels, on_device(): pl.pallas_call(functools.partial(kernel, rows_n, slabs_n, taps), out_shap...  106 us
    unnamed x11, local copies, waits for them, and re-layouts  4.9 us

profile of v2, /device:TPU:0, one launch (start us, length us, event | category | flops | bytes accessed | tf_op | source)
XLA Modules:
  0.0 110.5 jit_solution(10770964311454862338)
XLA Ops:
  0.0 0.0 copy-start
  0.0 1.2 %copy-done = f32[16,64,256]{2,1,0:T(8,128)S(1)} copy-done((f32[16,64,256]{2,1,0:T(8,128)S(1)}, f32[16,64,256]{2,1,0:T(8,128)}, u32[]{:S(2)}) %copy-start) | copy-done | bytes 1048600
  1.2 0.0 copy-start.1
  1.2 0.7 copy-done.1
  1.9 0.0 copy-start.2
  1.9 0.7 copy-done.2
  2.6 0.0 copy-start.3
  2.6 0.7 copy-done.3
  3.3 0.0 copy-start.4
  3.3 0.7 copy-done.4
  3.9 105.6 %shard_map.55 = f32[16,64,256]{2,1,0:T(8,128)S(1)} custom-call(s32[16]{0:T(128)S(1)} %copy-done.3, f32[31]{0:T(128)S(1)} %copy-done.4, f32[16,31]{1,0:T(8,128)S(1)} %copy-done.1, f32[16,31]{1,0:T(8,128)S(1)} %copy-done.2, f32[16,64,256]{2,1,0:T(8,128)S(1)} %copy-done), custom_call_target="tpu_custom_call" | custom-call | tf_op jit(solution)/shard_map/pallas_call | solution.py:348
  109.6 1.0 copy.7
Async XLA Ops:
  0.0 1.2 %copy-start = (f32[16,64,256]{2,1,0:T(8,128)S(1)}, f32[16,64,256]{2,1,0:T(8,128)}, u32[]{:S(2)}) copy-start(f32[16,64,256]{2,1,0:T(8,128)} %obs_ref.1) | copy-start | bytes 3145732
  1.2 0.7 copy-start.1
  1.9 0.7 copy-start.2
  2.6 0.7 copy-start.3
  3.3 0.7 copy-start.4

commit v3 on v2

--- a/solution.py
+++ b/solution.py
@@ -19,26 +19,43 @@
     return high, (v - high.astype(F32)).astype(BF16)
 
 
-def chunk_order(count):
-    if count < 4:
-        return list(range(count))
-    return [1, 0, count - 1] + list(range(2, count - 1))
+def chunk_order(count, it):
+    first = [1, 0] if it == 0 else [0, 1]
+    inner = list(range(2, count - 1))
+    return first + ([count - 1] + inner if it == ITERS - 1 else inner + [count - 1])
 
 
 def kernel(
     rows_n, slabs_n, taps,
-    band_ref, tz_ref, tx_ref, ty_ref, obs_ref,
+    band_hbm, tz_hbm, tx_hbm, ty_hbm, obs_hbm,
     out_ref,
+    band_ref, tz_ref, tx_ref, ty_ref, in_sem,
     txf_ref, txr_ref, tyf_ref, tyr_ref, ext, dext, bz, rz, wf_h, wf_l, wa_h, wa_l, af, aa,
     zs_sem, zr_sem, xs_sem, xr_sem,
 ):
-    depth, height, width = obs_ref.shape
+    depth, height, width = obs_hbm.shape
     radius = taps // 2
     halo = CHUNK
     chunks = height // CHUNK
-    order = chunk_order(chunks)
     row = lax.axis_index("row")
     slab = lax.axis_index("slab")
+    parity = row % 2
+
+    def chunk(p):
+        return p + parity * (chunks - 1 - 2 * p)
+
+    def begin(p, more=0, unit=CHUNK):
+        return pl.multiple_of(chunk(p) * CHUNK + more, unit)
+
+    fetches = [
+        pltpu.make_async_copy(src, dst, in_sem.at[n])
+        for n, (src, dst) in enumerate((
+            (obs_hbm, ext.at[0, :, pl.ds(halo, height), :]),
+            (ty_hbm, ty_ref), (tx_hbm, tx_ref), (band_hbm, band_ref), (tz_hbm, tz_ref),
+        ))
+    ]
+    for fetch in fetches:
+        fetch.start()
 
     sides = {
         ("row", 0): (row < rows_n - 1, row + 1),
@@ -85,7 +102,7 @@
             src_start, dst_start = depth, 0
         else:
             src_start, dst_start = radius, radius + depth
-        span = pl.ds(c * CHUNK, CHUNK)
+        span = pl.ds(begin(c), CHUNK)
         return pltpu.make_async_remote_copy(
             src_ref=buf.at[it, pl.ds(src_start, radius), span, :],
             dst_ref=buf.at[it, pl.ds(dst_start, radius), span, :],
@@ -95,13 +112,13 @@
             device_id_type=pl.DeviceIdType.MESH,
         )
 
-    def start(axis, side, make):
-        @pl.when(sides[(axis, side)][0])
+    def start(axis, side, make, also=True):
+        @pl.when(sides[(axis, side)][0] & also)
         def _():
             make(side).start()
 
-    def recv(axis, side, make):
-        @pl.when(sides[(axis, 1 - side)][0])
+    def recv(axis, side, make, also=True):
+        @pl.when(sides[(axis, 1 - side)][0] & also)
         def _():
             make(side).wait_recv()
 
@@ -113,17 +130,24 @@
     sends = []
 
     def x_make(it, which):
-        if which == 0:
-            src = (obs_ref, 0) if it == 0 else (ext.at[it], halo)
-            return functools.partial(row_copy, src, ext, it, which)
-        return functools.partial(row_copy, (dext.at[it], halo), dext, it, which)
+        buffer = ext if which == 0 else dext
+        return functools.partial(row_copy, (buffer.at[it], halo), buffer, it, which)
 
     def z_make(it, which, c):
         return functools.partial(slab_copy, bz if which == 0 else rz, it, which, c)
 
-    def x_start(it, which, side):
-        start("row", side, x_make(it, which))
-        sends.append(("row", side, x_make(it, which)))
+    def x_start(it, which, p):
+        near = p == 0
+        for v in range(2):
+            side = 1 - v if near else v
+            start("row", side, x_make(it, which), parity == v)
+        if near:
+            sends.extend(("row", side, x_make(it, which)) for side in range(2))
+
+    def x_recv(it, which, p):
+        near = p == 0
+        for v in range(2):
+            recv("row", v if near else 1 - v, x_make(it, which), parity == v)
 
     def z_start(it, which, c):
         for side in range(2):
@@ -134,10 +158,11 @@
         for side in range(2):
             recv("slab", side, z_make(it, which, c))
 
-    for side in range(2):
-        x_start(0, 0, side)
-
-    ext[0, :, halo:halo + height, :] = obs_ref[...]
+    fetches[0].wait()
+    for p in (0, chunks - 1):
+        x_start(0, 0, p)
+    for fetch in fetches[1:]:
+        fetch.wait()
 
     kk = 3 * halo
     mirror = (
@@ -220,12 +245,20 @@
         both = jnp.dot(jnp.concatenate([high, low], axis=0), w_h, preferred_element_type=F32)
         return both[:n] + both[n:] + jnp.dot(high, w_l, preferred_element_type=F32)
 
-    def stage_xy(it, c):
+    def edge(it, which, p):
+        if p in (0, chunks - 1):
+            x_recv(it, which, p)
+
+    def stage_xy(it, p):
+        edge(it, 0, p)
+        c = begin(p)
+
         def body(z, carry):
-            v = blur_rows(af[z], ext[it, z, c * CHUNK:c * CHUNK + kk, :])
-            bz[it, radius + z, c * CHUNK:(c + 1) * CHUNK, :] = blur_columns(v, wf_h[z], wf_l[z])
+            v = blur_rows(af[z], ext[it, z, pl.ds(c, kk), :])
+            bz[it, radius + z, pl.ds(c, CHUNK), :] = blur_columns(v, wf_h[z], wf_l[z])
             return carry
         lax.fori_loop(0, depth, body, 0, unroll=4)
+        z_start(it, 0, p)
 
     def blur_depth(buf, it, tile, lanes, flip):
         total = None
@@ -235,64 +268,52 @@
             total = term if total is None else total + term
         return total
 
-    def tiles(c):
-        for r in range(CHUNK // 8):
-            for l in range(width // 128):
-                yield slice(c * CHUNK + r * 8, c * CHUNK + r * 8 + 8), slice(l * 128, l * 128 + 128)
-
-    def stage_ratio(it, c):
-        for tile, lanes in tiles(c):
-            rz[it, radius:radius + depth, tile, lanes] = obs_ref[:, tile, lanes] / blur_depth(bz, it, tile, lanes, False)
-
-    def stage_zy(it, c):
-        inner = slice(halo + c * CHUNK, halo + (c + 1) * CHUNK)
-        for tile, lanes in tiles(c):
-            target = slice(halo + tile.start, halo + tile.stop)
-            dext[it, :, target, lanes] = blur_depth(rz, it, tile, lanes, True)
+    def tiles(p):
+        for r in range(0, CHUNK, 8):
+            for l in range(0, width, LANES):
+                yield pl.ds(begin(p, r, 8), 8), pl.ds(begin(p, halo + r, 8), 8), slice(l, l + LANES)
+
+    def stage_ratio(it, p):
+        for tile, inner, lanes in tiles(p):
+            blurred = blur_depth(bz, it, tile, lanes, False)
+            rz[it, radius:radius + depth, tile, lanes] = ext[0, :, inner, lanes] / blurred
+        z_start(it, 1, p)
+
+    def stage_zy(it, p):
+        for tile, inner, lanes in tiles(p):
+            dext[it, :, inner, lanes] = blur_depth(rz, it, tile, lanes, True)
+        rows = pl.ds(begin(p, halo), CHUNK)
 
         def body(z, carry):
-            dext[it, z, inner, :] = blur_columns(dext[it, z, inner, :], wa_h[z], wa_l[z])
+            dext[it, z, rows, :] = blur_columns(dext[it, z, rows, :], wa_h[z], wa_l[z])
             return carry
         lax.fori_loop(0, depth, body, 0, unroll=4)
-
-    def stage_x(it, c):
-        span = slice(c * CHUNK, (c + 1) * CHUNK)
-        inner = slice(halo + c * CHUNK, halo + (c + 1) * CHUNK)
+        if p in (0, chunks - 1):
+            x_start(it, 1, p)
+
+    def stage_x(it, p):
+        edge(it, 1, p)
+        c = begin(p)
+        inner = pl.ds(begin(p, halo), CHUNK)
 
         def body(z, carry):
-            v = ext[it, z, inner, :] * blur_rows(aa[z, c], dext[it, z, c * CHUNK:c * CHUNK + kk, :])
+            v = ext[it, z, inner, :] * blur_rows(aa[z, chunk(p)], dext[it, z, pl.ds(c, kk), :])
             if it == ITERS - 1:
-                out_ref[z, span, :] = v
+                out_ref[z, pl.ds(c, CHUNK), :] = v
             else:
                 ext[it + 1, z, inner, :] = v
             return carry
         lax.fori_loop(0, depth, body, 0, unroll=4)
+        if it < ITERS - 1 and p in (0, chunks - 1):
+            x_start(it + 1, 0, p)
 
     clear("row", ext, 0)
     lax.fori_loop(0, depth, build_forward, 0, unroll=2)
+    started = 0
     for it in range(ITERS):
-        def edge_x(which, c, it=it):
-            if c == 0:
-                recv("row", 0, x_make(it, which))
-            if c == chunks - 1:
-                recv("row", 1, x_make(it, which))
-
-        def back_x(c, it=it, edge_x=edge_x):
-            edge_x(1, c)
-            stage_x(it, c)
-            if it < ITERS - 1:
-                if c == 0:
-                    x_start(it + 1, 0, 1)
-                if c == chunks - 1:
-                    x_start(it + 1, 0, 0)
-
-        for n, c in enumerate(order):
-            edge_x(0, c)
-            stage_xy(it, c)
-            z_start(it, 0, c)
-            if n == 0 and it > 0:
-                for extra in late:
-                    late_x(extra)
+        order = chunk_order(chunks, it)
+        for p in order[started:]:
+            stage_xy(it, p)
         if it == 0:
             lax.fori_loop(0, depth, build_adjoint, 0)
             for buffer in (bz, rz):
@@ -302,33 +323,32 @@
                 clear("row", dext, i)
             for i in range(1, ITERS):
                 clear("row", ext, i)
-        for c in order:
-            z_recv(it, 0, c)
-            stage_ratio(it, c)
-            z_start(it, 1, c)
-        done, left = [], list(range(chunks))
-        for n, c in enumerate(order):
-            if n == chunks - 1:
-                for e in list(left):
-                    if all(near in done for near in (e - 1, e, e + 1) if 0 <= near < chunks):
-                        back_x(e)
-                        left.remove(e)
-            z_recv(it, 1, c)
-            stage_zy(it, c)
-            done.append(c)
-            if c == 0:
-                x_start(it, 1, 1)
-            if c == chunks - 1:
-                x_start(it, 1, 0)
-        needed = [e for e in left if abs(e - order[0]) <= 1]
-        late = [e for e in left if e not in needed]
-        late_x = back_x
-        for e in needed:
-            back_x(e)
-        if it == ITERS - 1 or order[0] in (0, chunks - 1):
-            for e in late:
-                back_x(e)
-            late = []
+        for p in order:
+            z_recv(it, 0, p)
+            stage_ratio(it, p)
+        for p in order[:-1]:
+            z_recv(it, 1, p)
+            stage_zy(it, p)
+        if it < ITERS - 1:
+            for p in range(chunks - 2):
+                stage_x(it, p)
+            for p in range(chunks - 3):
+                stage_xy(it + 1, p)
+            z_recv(it, 1, order[-1])
+            stage_zy(it, order[-1])
+            stage_x(it, chunks - 2)
+            stage_xy(it + 1, chunks - 3)
+            stage_x(it, chunks - 1)
+            started = chunks - 2
+        else:
+            early = [p for p in range(chunks) if abs(p - order[-1]) > 1]
+            for p in early:
+                stage_x(it, p)
+            z_recv(it, 1, order[-1])
+            stage_zy(it, order[-1])
+            for p in range(chunks):
+                if p not in early:
+                    stage_x(it, p)
 
     for axis, side, make in sends:
         sent(axis, side, make)
@@ -343,14 +363,20 @@
         radius = taps // 2
 
         vmem = pl.BlockSpec(memory_space=pltpu.VMEM)
-        smem = pl.BlockSpec(memory_space=pltpu.SMEM)
+        hbm = pl.BlockSpec(memory_space=pltpu.HBM)
         chunks = height // CHUNK
         return pl.pallas_call(
             functools.partial(kernel, rows_n, slabs_n, taps),
             out_shape=jax.ShapeDtypeStruct(observed.shape, F32),
-            in_specs=[smem, smem] + [vmem] * 3,
+            in_specs=[hbm] * 5,
             out_specs=vmem,
-            scratch_shapes=[pltpu.VMEM((bands, LANES), F32)] * 4 + [
+            scratch_shapes=[
+                pltpu.SMEM((depth,), jnp.int32),
+                pltpu.SMEM((taps,), F32),
+                pltpu.VMEM((bands, taps), F32),
+                pltpu.VMEM((bands, taps), F32),
+                pltpu.SemaphoreType.DMA((5,)),
+            ] + [pltpu.VMEM((bands, LANES), F32)] * 4 + [
                 pltpu.VMEM((ITERS, depth, height + 2 * CHUNK, width), F32),
                 pltpu.VMEM((ITERS, depth, height + 2 * CHUNK, width), F32),
                 pltpu.VMEM((ITERS, depth + 2 * radius, height, width), F32),
@@ -367,7 +393,7 @@
                 pltpu.SemaphoreType.DMA((ITERS, 2, 2)),
             ],
             compiler_params=pltpu.CompilerParams(
-                collective_id=0, has_side_effects=True, vmem_limit_bytes=40 * 1024 * 1024
+                collective_id=0, has_side_effects=True, vmem_limit_bytes=63 * 1024 * 1024 + 900 * 1024
             ),
         )(
             band_index, taps_z, taps_x, taps_y,

time: 111 us -> 106 us (0.955)
  Pallas kernels: 106 us -> 103 us
  local copies, waits for them, and re-layouts: 4.9 us -> 2.29 us
    unnamed x11 -> x1, local copies, waits for them, and re-layouts: 4.9 us -> 2.29 us
    pallas_call x1, Pallas kernels: 106 us -> 103 us  [on_device(): pl.pallas_call(functools.partial(kernel, rows_n, slabs_n, taps), out_shap...]
where the time goes in v3:
time: 106 us
  Pallas kernels  103 us (97%)
  local copies, waits for them, and re-layouts  2.29 us (2%)
    pallas_call x1, Pallas kernels, on_device(): pl.pallas_call(functools.partial(kernel, rows_n, slabs_n, taps), out_shap...  103 us
    unnamed x1, local copies, waits for them, and re-layouts  2.29 us

profile of v3, /device:TPU:0, one launch (start us, length us, event | category | flops | bytes accessed | tf_op | source)
XLA Modules:
  0.0 105.5 jit_solution(8344209320323461949)
XLA Ops:
  0.0 103.2 %shard_map.55 = f32[16,64,256]{2,1,0:T(8,128)} custom-call(s32[16]{0:T(128)} %band_hbm.1, f32[31]{0:T(128)} %tz_hbm.1, f32[16,31]{1,0:T(8,128)} %tx_hbm.1, f32[16,31]{1,0:T(8,128)} %ty_hbm.1, f32[16,64,256]{2,1,0:T(8,128)} %obs_hbm.1), custom_call_target="tpu_custom_call" | custom-call | tf_op jit(solution)/shard_map/pallas_call | solution.py:368
  103.2 2.3 %copy.7 = f32[16,64,256]{2,1,0:T(8,128)} copy(f32[16,64,256]{2,1,0:T(8,128)} %shard_map.55) | data formatting | bytes 2097152

commit v4 on v3

--- a/solution.py
+++ b/solution.py
@@ -257,7 +257,7 @@
             v = blur_rows(af[z], ext[it, z, pl.ds(c, kk), :])
             bz[it, radius + z, pl.ds(c, CHUNK), :] = blur_columns(v, wf_h[z], wf_l[z])
             return carry
-        lax.fori_loop(0, depth, body, 0, unroll=4)
+        lax.fori_loop(0, depth, body, 0, unroll=8)
         z_start(it, 0, p)
 
     def blur_depth(buf, it, tile, lanes, flip):
@@ -287,7 +287,7 @@
         def body(z, carry):
             dext[it, z, rows, :] = blur_columns(dext[it, z, rows, :], wa_h[z], wa_l[z])
             return carry
-        lax.fori_loop(0, depth, body, 0, unroll=4)
+        lax.fori_loop(0, depth, body, 0, unroll=8)
         if p in (0, chunks - 1):
             x_start(it, 1, p)
 
@@ -303,7 +303,7 @@
             else:
                 ext[it + 1, z, inner, :] = v
             return carry
-        lax.fori_loop(0, depth, body, 0, unroll=4)
+        lax.fori_loop(0, depth, body, 0, unroll=8)
         if it < ITERS - 1 and p in (0, chunks - 1):
             x_start(it + 1, 0, p)
 

time: 106 us -> 104 us (0.981)
  Pallas kernels: 103 us -> 101 us
    pallas_call x1, Pallas kernels: 103 us -> 101 us  [on_device(): pl.pallas_call(functools.partial(kernel, rows_n, slabs_n, taps), out_shap...]
where the time goes in v4:
time: 104 us; the launch traced here: 103 us
  Pallas kernels  101 us (97%)
  local copies, waits for them, and re-layouts  2.29 us (2%)
    pallas_call x1, Pallas kernels, on_device(): pl.pallas_call(functools.partial(kernel, rows_n, slabs_n, taps), out_shap...  101 us
    unnamed x1, local copies, waits for them, and re-layouts  2.29 us

profile of v4, /device:TPU:0, one launch (start us, length us, event | category | flops | bytes accessed | tf_op | source)
XLA Modules:
  0.0 103.4 jit_solution(13787758152410399107)
XLA Ops:
  0.0 101.1 %shard_map.55 = f32[16,64,256]{2,1,0:T(8,128)} custom-call(s32[16]{0:T(128)} %band_hbm.1, f32[31]{0:T(128)} %tz_hbm.1, f32[16,31]{1,0:T(8,128)} %tx_hbm.1, f32[16,31]{1,0:T(8,128)} %ty_hbm.1, f32[16,64,256]{2,1,0:T(8,128)} %obs_hbm.1), custom_call_target="tpu_custom_call" | custom-call | tf_op jit(solution)/shard_map/pallas_call | solution.py:368
  101.1 2.3 %copy.7 = f32[16,64,256]{2,1,0:T(8,128)} copy(f32[16,64,256]{2,1,0:T(8,128)} %shard_map.55) | data formatting | bytes 2097152
